TPU v7x, 32 devices: a whole 2x2x4 slice. The times are simulated.
32 devices in a mesh: grp: 2 (over y), leaf: 16 (over z, x, core).
Axes of the slice: x: 2, y: 2, z: 4, core: 2. Of those that a mesh axis runs over, the one named last changes fastest.
Arguments:
- vectors: float32 [16, 32768], P(None, ('grp', 'leaf')), may hold values from -6 to 6
- points: float32 [3, 32768], P(None, ('grp', 'leaf')), may hold values from -1 to 2
- near_lists: int32 [64, 6], P(('grp', 'leaf')), may hold values from -1 to 5, as said below
- inter_lists: int32 [64, 16], P(('grp', 'leaf')), may hold values from 0 to 31, as said below
- skeleton: int32 [64, 64], P(('grp', 'leaf')), may hold values from 0 to 511, as said below
- interp: float32 [64, 64, 512], P(('grp', 'leaf')), may hold values from -0.25 to 0.25
- transfer: float32 [64, 64, 128], P(('grp', 'leaf')), may hold values from -0.125 to 0.125
- coarse_points: float32 [2, 3, 128], replicated, may hold values from 0 to 1
Outputs:
- filtered: float32 [16, 32768], P(None, ('grp', 'leaf'))
Inputs may be any that keep to these rules, and one draw needn't show every extreme that they name: `near_lists`: place w of leaf l's window is leaf (l // 2 - 1) * 2 + w. Slot 0 holds the leaf itself (2 + l % 2); the next slots hold distinct places of other leaves of the same subtree; then -1 to the end of the row. `inter_lists`: distinct leaves of the leaf's own subtree, numbered from the subtree's first leaf, none in the leaf's window. `skeleton`: distinct places within the leaf.
All inputs are finite; a program needn't handle non-finite values.
Results may differ from a plain program's by a relative error of at most 0.00013.
Values sent between devices are 32-bit elements; how exact they have to be, the bound alone decides.
No kernel may reach another device: no remote copies, remote signals or barrier semaphores. Data moves between devices by JAX's collectives and lax.ppermute only.
A program may use at most 64 MiB of HBM per device.

v0:
```python
import jax
import jax.numpy as jnp
from jax import lax
from jax.sharding import PartitionSpec as P

kappa_scale = 3.4641016151377544
centre = 0.05
half_width = 0.05
highest = lax.Precision.HIGHEST


def with_halo(x, sides, width):
    for axis, dim in sides:
        devices, length = (lax.axis_size(axis), x.shape[dim])
        up = [(i, (i + 1) % devices) for i in range(devices - 1)]
        down = [(j, i) for i, j in up]
        last = lax.slice_in_dim(x, length - width, length, axis=dim)
        initial = lax.slice_in_dim(x, 0, width, axis=dim)
        before = lax.ppermute(last, axis, up)
        after = lax.ppermute(initial, axis, down)
        x = jnp.concatenate([before, x, after], axis=dim)
    return x


def matern(source, target):
    delta_x = source[..., 0, :, None] - target[..., 0, None, :]
    delta_y = source[..., 1, :, None] - target[..., 1, None, :]
    delta_z = source[..., 2, :, None] - target[..., 2, None, :]
    scaled = kappa_scale * jnp.sqrt(delta_x * delta_x + delta_y * delta_y + delta_z * delta_z)
    return (1.0 + scaled) * jnp.exp(-scaled)


def on_device(vectors, points, near_lists, inter_lists, skeleton, interp, transfer, coarse_points):
    per_dev = near_lists.shape[0]
    slot_count = near_lists.shape[1]
    leaf_size = interp.shape[2]
    vec_count = vectors.shape[0]
    leaf_index = lax.axis_index("leaf")
    group_index = lax.axis_index("grp")
    group_count = lax.axis_size("grp")
    leaf_points = points.reshape(3, per_dev, leaf_size).transpose(1, 0, 2)
    skel_points = jnp.take_along_axis(leaf_points, skeleton[:, None, :], axis=2)
    subtree_skel = lax.all_gather(skel_points, "leaf", axis=0, tiled=True)
    own_coarse = lax.dynamic_index_in_dim(coarse_points, group_index, 0, keepdims=False)
    apart = (jnp.arange(group_count) != group_index).astype(jnp.float32)
    coupling = matern(coarse_points, own_coarse[None]) * apart[:, None, None]
    live_slots = jnp.max(jnp.sum((near_lists >= 0).astype(jnp.int32), axis=1))
    first_leaf = leaf_index * per_dev
    subtree_lists = lax.all_gather(inter_lists, "leaf", axis=0, tiled=True)
    own_ids = first_leaf + jnp.arange(per_dev, dtype=jnp.int32)
    hits = jnp.sum(
        (subtree_lists[:, :, None] == own_ids[None, None, :]).astype(jnp.float32), axis=1
    )
    push_kernel = matern(skel_points[None], subtree_skel[:, None]) * hits[:, :, None, None]

    def operate(field):
        stacked = jnp.concatenate([points, field], axis=0)
        window = with_halo(stacked, (("leaf", 1),), per_dev * leaf_size)
        window_points = window[:3].reshape(3, 3 * per_dev, leaf_size)
        window_vecs = window[3:].reshape(vec_count, 3 * per_dev, leaf_size)

        def near_slot(slot, running):
            chosen = lax.dynamic_index_in_dim(near_lists, slot, 1, keepdims=False)
            present = (chosen >= 0).astype(jnp.float32)
            safe_place = jnp.where(chosen >= 0, chosen, 0)
            source_points = jnp.take(window_points, safe_place, axis=1).transpose(1, 0, 2)
            source_vecs = jnp.take(window_vecs, safe_place, axis=1)
            kernel = matern(source_points, leaf_points)
            product = jnp.einsum("vlp,lpq->lvq", source_vecs, kernel, precision=highest)
            return running + present[:, None, None] * product

        near_part = lax.fori_loop(
            0, live_slots, near_slot, jnp.zeros((per_dev, vec_count, leaf_size), jnp.float32)
        )
        leaf_vecs = field.reshape(vec_count, per_dev, leaf_size)
        coeffs = jnp.einsum("vlp,lrp->lvr", leaf_vecs, interp, precision=highest)
        leaf_far = lax.psum_scatter(
            jnp.einsum("jvr,tjrq->tvq", coeffs, push_kernel, precision=highest),
            "leaf",
            scatter_dimension=0,
            tiled=True,
        )
        upward = jnp.einsum("lvr,lrc->vc", coeffs, transfer, precision=highest)
        subtree_total = lax.psum(upward, "leaf")
        group_coeffs = lax.all_gather(subtree_total[None], "grp", axis=0, tiled=True)
        coarse_field = jnp.einsum("avr,arq->vq", group_coeffs, coupling, precision=highest)
        downward = leaf_far + jnp.einsum("vc,lrc->lvr", coarse_field, transfer, precision=highest)
        far_part = jnp.einsum("lvr,lrp->lvp", downward, interp, precision=highest)
        combined = (near_part + far_part) / (leaf_size * slot_count)
        return combined.transpose(1, 0, 2).reshape(vec_count, per_dev * leaf_size)

    term_one = (operate(vectors) - centre * vectors) / half_width
    term_two = 2.0 * (operate(term_one) - centre * term_one) / half_width - vectors
    term_three = 2.0 * (operate(term_two) - centre * term_two) / half_width - term_one
    squares = lax.psum(jnp.sum(term_three * term_three, axis=1), ("grp", "leaf"))
    total_points = vectors.shape[1] * group_count * lax.axis_size("leaf")
    return term_three / jnp.sqrt(squares / total_points + 1e-06)[:, None]


def solution(mesh):
    placed = (
        P(None, ("grp", "leaf")),
        P(None, ("grp", "leaf")),
        P(("grp", "leaf"), None),
        P(("grp", "leaf"), None),
        P(("grp", "leaf"), None),
        P(("grp", "leaf"), None, None),
        P(("grp", "leaf"), None, None),
        P(),
    )
    return jax.shard_map(
        on_device, mesh=mesh, in_specs=placed, out_specs=P(None, ("grp", "leaf")), check_vma=False
    )
```

profile of v0, /device:TPU:10, one launch (start us, length us, event | category | flops | bytes accessed | tf_op | source)
XLA Modules:
  0.0 312.5 jit_solution(3287674258489741425)
XLA Ops:
  6.5 0.9 pad_maximum_fusion.3
  7.5 2.1 collective-permute-start.1
  9.5 2.4 collective-permute-start
  11.9 0.9 copy.61
  13.0 1.2 gather_fusion.6
  14.4 15.5 %all-gather = s32[16,2,16]{2,1,0:T(2,128)S(1)} all-gather(s32[1,2,16]{2,1,0:T(2,128)S(1)} %bitcast.260), channel_id=1, replica_groups=mesh['grp'=2,'leaf'=16] {'leaf'}, dimensions={0}, use_global_device_ids=true | all-gather | bytes 2176 | tf_op jit(solution)/shard_map/all_gather | solution.py:49
  30.1 21.1 %all_gather.15 = f32[32,3,64]{2,1,0:T(4,128)S(1)} all-gather(f32[2,3,64]{2,1,0:T(4,128)S(1)} %bitcast_select_fusion.1), channel_id=1, replica_groups=mesh['grp'=2,'leaf'=16] {'leaf'}, dimensions={0}, use_global_device_ids=true | all-gather | bytes 26112 | tf_op jit(solution)/shard_map/all_gather | solution.py:43
  51.6 3.5 %convolution_bitcast_fusion.2 = f32[32,16,64]{2,1,0:T(8,128)} fusion(f32[32,2]{1,0:T(8,128)S(1)} %copy.67, f32[32,64]{1,0:T(8,128)S(1)} %bitcast.254, f32[2,64]{1,0:T(2,128)S(1)} %bitcast.264, f32[32,64]{1,0:T(8,128)S(1)} %bitcast.257, f32[2,64]{1,0:T(2,128)S(1)} %bitcast.267, f32[32,64]{1,0:T(8,128)S(1)} %bitcast.251, f32[2,64]{1,0:T(2,128)S(1)} %bitcast.261, ...), kind=kOutput, calls=%fused_computation.145 | convolution fusion | flops 53739520 | bytes 165632 | tf_op jit(solution)/shard_map/jvr,tjrq->tvq/dot_general | solution.py:78
  56.1 24.3 %psum.28 = f32[1,16,128]{2,1,0:T(8,128)S(1)} all-reduce(f32[1,16,128]{2,1,0:T(8,128)S(1)} %convolution_bitcast_fusion.8), channel_id=1, replica_groups=mesh['grp'=2,'leaf'=16] {'leaf'}, use_global_device_ids=true, to_apply=%region_6.9 | all-reduce | flops 2048 | bytes 16384 | tf_op jit(solution)/shard_map/psum | solution.py:84
  80.4 4.4 %all_gather.17 = f32[2,16,128]{2,1,0:T(8,128)S(1)} all-gather(f32[1,16,128]{2,1,0:T(8,128)S(1)} %psum.28), channel_id=1, replica_groups=mesh['grp'=2,'leaf'=16] {'grp'}, dimensions={0}, use_global_device_ids=true | all-gather | bytes 24576 | tf_op jit(solution)/shard_map/all_gather | solution.py:85
  85.3 0.6 reduce_max.9
  86.1 28.6 %while.30 = (s32[]{:T(128)}, f32[2,16,512]{2,1,0:T(8,128)S(1)}, s32[]{:T(128)}, s32[2,6]{0,1:T(8,128)S(1)}, f32[16,6,512]{2,0,1:T(8,128)S(1)}, /*index=5*/f32[3,...) while((s32[]{:T(128)}, f32[2,16,512]{2,1,0:T(8,128)S(1)}, s32[]{:T(128)}, ...), condition=%wide.region_3.0_spmd, body=%wide.region_2.0_spmd.sunk | while | flops 107008024 | bytes 479441 | solution.py:72
  87.9 2.8 fusion.199
  92.6 2.8 fusion.199
  97.3 2.8 fusion.199
  102.0 2.8 fusion.199
  106.6 2.8 fusion.199
  111.3 2.8 fusion.199
  114.7 0.9 fusion.116
  116.0 1.9 collective-permute-start.3
  117.9 2.4 collective-permute-start.2
  120.7 3.5 %convolution_bitcast_fusion.1 = f32[32,16,64]{2,1,0:T(8,128)} fusion(f32[32,2]{1,0:T(8,128)S(1)} %copy.67, f32[32,64]{1,0:T(8,128)S(1)} %bitcast.255, f32[2,64]{1,0:T(2,128)S(1)} %bitcast.265, f32[32,64]{1,0:T(8,128)S(1)} %bitcast.258, f32[2,64]{1,0:T(2,128)S(1)} %bitcast.268, f32[32,64]{1,0:T(8,128)S(1)} %bitcast.252, f32[2,64]{1,0:T(2,128)S(1)} %bitcast.262, ...), kind=kOutput, calls=%fused_computation.144 | convolution fusion | flops 53739520 | bytes 165632 | tf_op jit(solution)/shard_map/jvr,tjrq->tvq/dot_general | solution.py:78
  124.4 26.7 %psum.29 = f32[1,16,128]{2,1,0:T(8,128)S(1)} all-reduce(f32[1,16,128]{2,1,0:T(8,128)S(1)} %convolution_bitcast_fusion.7), channel_id=1, replica_groups=mesh['grp'=2,'leaf'=16] {'leaf'}, use_global_device_ids=true, to_apply=%region_10.13 | all-reduce | flops 2048 | bytes 16384 | tf_op jit(solution)/shard_map/psum | solution.py:84
  151.2 4.4 %all_gather.18 = f32[2,16,128]{2,1,0:T(8,128)S(1)} all-gather(f32[1,16,128]{2,1,0:T(8,128)S(1)} %psum.29), channel_id=1, replica_groups=mesh['grp'=2,'leaf'=16] {'grp'}, dimensions={0}, use_global_device_ids=true | all-gather | bytes 24576 | tf_op jit(solution)/shard_map/all_gather | solution.py:85
  156.0 28.8 %while.31 = (s32[]{:T(128)}, f32[2,16,512]{2,1,0:T(8,128)S(1)}, s32[]{:T(128)}, s32[2,6]{0,1:T(8,128)S(1)}, f32[16,6,512]{2,0,1:T(8,128)S(1)}, /*index=5*/f32[3,...) while((s32[]{:T(128)}, f32[2,16,512]{2,1,0:T(8,128)S(1)}, s32[]{:T(128)}, ...), condition=%wide.region_8.11_spmd, body=%wide.region_7.10_spmd.sunk | while | flops 107008024 | bytes 479441 | solution.py:72
  158.1 2.8 fusion.203
  162.7 2.8 fusion.203
  167.4 2.8 fusion.203
  172.1 2.8 fusion.203
  176.8 2.8 fusion.203
  181.4 2.8 fusion.203
  185.3 0.9 fusion.115
  186.6 1.9 collective-permute-start.5
  188.5 2.4 collective-permute-start.4
  191.3 3.5 %convolution_bitcast_fusion = f32[32,16,64]{2,1,0:T(8,128)} fusion(f32[32,2]{1,0:T(8,128)S(1)} %copy.67, f32[32,64]{1,0:T(8,128)S(1)} %bitcast.256, f32[2,64]{1,0:T(2,128)S(1)} %bitcast.266, f32[32,64]{1,0:T(8,128)S(1)} %bitcast.259, f32[2,64]{1,0:T(2,128)S(1)} %bitcast.269, f32[32,64]{1,0:T(8,128)S(1)} %bitcast.253, f32[2,64]{1,0:T(2,128)S(1)} %bitcast.263, ...), kind=kOutput, calls=%fused_computation.143 | convolution fusion | flops 53739520 | bytes 165632 | tf_op jit(solution)/shard_map/jvr,tjrq->tvq/dot_general | solution.py:78
  195.0 28.1 %psum.30 = f32[1,16,128]{2,1,0:T(8,128)S(1)} all-reduce(f32[1,16,128]{2,1,0:T(8,128)S(1)} %convolution_bitcast_fusion.6), channel_id=1, replica_groups=mesh['grp'=2,'leaf'=16] {'leaf'}, use_global_device_ids=true, to_apply=%region_14.17 | all-reduce | flops 2048 | bytes 16384 | tf_op jit(solution)/shard_map/psum | solution.py:84
  223.1 4.4 %all_gather.19 = f32[2,16,128]{2,1,0:T(8,128)S(1)} all-gather(f32[1,16,128]{2,1,0:T(8,128)S(1)} %psum.30), channel_id=1, replica_groups=mesh['grp'=2,'leaf'=16] {'grp'}, dimensions={0}, use_global_device_ids=true | all-gather | bytes 24576 | tf_op jit(solution)/shard_map/all_gather | solution.py:85
  227.9 28.6 %while.32 = (s32[]{:T(128)}, f32[2,16,512]{2,1,0:T(8,128)S(1)}, s32[]{:T(128)}, s32[2,6]{0,1:T(8,128)S(1)}, f32[16,6,512]{2,0,1:T(8,128)S(1)}, /*index=5*/f32[3,...) while((s32[]{:T(128)}, f32[2,16,512]{2,1,0:T(8,128)S(1)}, s32[]{:T(128)}, ...), condition=%wide.region_12.15_spmd, body=%wide.region_11.14_spmd.sunk | while | flops 107008024 | bytes 479441 | solution.py:72
  229.8 2.8 fusion.207
  234.5 2.8 fusion.207
  239.2 2.8 fusion.207
  243.8 2.8 fusion.207
  248.5 2.8 fusion.207
  253.2 2.8 fusion.207
  256.6 0.7 reduce-scatter.8.cloned.1.call-done
  257.3 0.9 fusion.114
  258.7 46.5 %psum.31 = f32[16]{0:T(128)S(1)} all-reduce(f32[16]{0:T(128)S(1)} %multiply_reduce_fusion), channel_id=1, replica_groups=mesh['grp'=2,'leaf'=16] {'grp','leaf'}, use_global_device_ids=true, to_apply=%region_16.19 | all-reduce | flops 16 | bytes 128 | tf_op jit(solution)/shard_map/psum | solution.py:95
  305.2 0.7 broadcast_divide_fusion
  (228 shorter events, 28.3 us)
Async XLA Ops:
  6.5 44.8 %copy-start = (f32[2,64,512]{2,1,0:T(8,128)S(1)}, f32[2,64,512]{2,1,0:T(8,128)}, u32[]{:S(2)}) copy-start(f32[2,64,512]{2,1,0:T(8,128)} %param.23) | copy-start | bytes 786436
  6.5 6.4 %copy-start.7 = (s32[2,64]{1,0:T(2,128)S(1)}, s32[2,64]{1,0:T(2,128)}, u32[]{:S(2)}) copy-start(s32[2,64]{1,0:T(2,128)} %param.22) | copy-start | bytes 1540
  6.5 7.8 %copy-start.5 = (s32[2,16]{1,0:T(2,128)S(1)}, s32[2,16]{1,0:T(2,128)}, u32[]{:S(2)}) copy-start(s32[2,16]{1,0:T(2,128)} %param.21) | copy-start | bytes 388
  6.5 108.2 %reduce-scatter.4.cloned.1.call-start = ((), (), s32[]{:S(2)}) async-start(), calls=%async_computation.3 | async-start | bytes 278528 | tf_op jit(solution)/shard_map/reduce_scatter | solution.py:77
  7.5 43.8 %copy-start.2 = (f32[16,1024]{1,0:T(8,128)S(1)}, f32[16,1024]{1,0:T(8,128)}, u32[]{:S(2)}) copy-start(f32[16,1024]{1,0:T(8,128)} %param.18) | copy-start | bytes 196612
  7.5 78.5 %collective-permute-start.1 = (f32[19,1024]{1,0:T(8,128)S(1)}, f32[19,1024]{1,0:T(8,128)S(1)}, u32[]{:S(2)}, u32[]{:S(2)}) collective-permute-start(f32[19,1024]{1,0:T(8,128)S(1)} %pad_maximum_fusion.3), channel_id=1, source_target_pairs={{1,0},{2,1},{3,2},{4,3},{5,4},{6,5},{7,6},{8,7},{9,8},{10,9},{11,1... | collective-permute-start | bytes 233480 | tf_op jit(solution)/shard_map/ppermute | solution.py:20
  9.5 76.4 %collective-permute-start = (f32[19,1024]{1,0:T(8,128)S(1)}, f32[19,1024]{1,0:T(8,128)S(1)}, u32[]{:S(2)}, u32[]{:S(2)}) collective-permute-start(f32[19,1024]{1,0:T(8,128)S(1)} %pad_maximum_fusion.3), channel_id=1, source_target_pairs={{0,1},{1,2},{2,3},{3,4},{4,5},{5,6},{6,7},{7,8},{8,9},{9,10},{10,1... | collective-permute-start | bytes 233480 | tf_op jit(solution)/shard_map/ppermute | solution.py:19
  55.1 0.7 copy-start.6
  55.1 0.9 copy-start.1
  55.1 29.7 %copy-start.4 = (f32[2,3,128]{2,0,1:T(2,128)S(1)}, f32[2,3,128]{2,0,1:T(2,128)}, u32[]{:S(2)}) copy-start(f32[2,3,128]{2,0,1:T(2,128)} %param.25) | copy-start | bytes 9220
  55.1 30.8 %copy-start.3 = (f32[3,1024]{1,0:T(4,128)S(1)}, f32[3,1024]{1,0:T(4,128)}, u32[]{:S(2)}) copy-start(f32[3,1024]{1,0:T(4,128)} %param.19) | copy-start | bytes 36868
  55.1 130.2 %reduce-scatter.6.cloned.1.call-start = ((), (), s32[]{:S(2)}) async-start(), calls=%async_computation.4 | async-start | bytes 278528 | tf_op jit(solution)/shard_map/reduce_scatter | solution.py:77
  116.0 39.9 %collective-permute-start.3 = (f32[19,1024]{1,0:T(8,128)S(1)}, f32[19,1024]{1,0:T(8,128)S(1)}, u32[]{:S(2)}, u32[]{:S(2)}) collective-permute-start(f32[19,1024]{1,0:T(8,128)S(1)} %pad_maximum_fusion.4), channel_id=1, source_target_pairs={{1,0},{2,1},{3,2},{4,3},{5,4},{6,5},{7,6},{8,7},{9,8},{10,9},{11,1... | collective-permute-start | bytes 233480 | tf_op jit(solution)/shard_map/ppermute | solution.py:20
  117.9 38.0 %collective-permute-start.2 = (f32[19,1024]{1,0:T(8,128)S(1)}, f32[19,1024]{1,0:T(8,128)S(1)}, u32[]{:S(2)}, u32[]{:S(2)}) collective-permute-start(f32[19,1024]{1,0:T(8,128)S(1)} %pad_maximum_fusion.4), channel_id=1, source_target_pairs={{0,1},{1,2},{2,3},{3,4},{4,5},{5,6},{6,7},{7,8},{8,9},{9,10},{10,1... | collective-permute-start | bytes 233480 | tf_op jit(solution)/shard_map/ppermute | solution.py:19
  124.4 132.9 %reduce-scatter.8.cloned.1.call-start = ((), (), s32[]{:S(2)}) async-start(), calls=%async_computation.5 | async-start | bytes 278528 | tf_op jit(solution)/shard_map/reduce_scatter | solution.py:77
  186.6 41.2 %collective-permute-start.5 = (f32[19,1024]{1,0:T(8,128)S(1)}, f32[19,1024]{1,0:T(8,128)S(1)}, u32[]{:S(2)}, u32[]{:S(2)}) collective-permute-start(f32[19,1024]{1,0:T(8,128)S(1)} %pad_maximum_fusion.5), channel_id=1, source_target_pairs={{1,0},{2,1},{3,2},{4,3},{5,4},{6,5},{7,6},{8,7},{9,8},{10,9},{11,1... | collective-permute-start | bytes 233480 | tf_op jit(solution)/shard_map/ppermute | solution.py:20
  188.5 39.3 %collective-permute-start.4 = (f32[19,1024]{1,0:T(8,128)S(1)}, f32[19,1024]{1,0:T(8,128)S(1)}, u32[]{:S(2)}, u32[]{:S(2)}) collective-permute-start(f32[19,1024]{1,0:T(8,128)S(1)} %pad_maximum_fusion.5), channel_id=1, source_target_pairs={{0,1},{1,2},{2,3},{3,4},{4,5},{5,6},{6,7},{7,8},{8,9},{9,10},{10,1... | collective-permute-start | bytes 233480 | tf_op jit(solution)/shard_map/ppermute | solution.py:19
Sparse Core Ops, SparseCore 0:
  55.2 56.6 reduce-scatter.3
  124.5 60.7 reduce-scatter.5
  195.1 62.1 reduce-scatter.7
where the time goes:
time: 313 us; the launch traced here: 312 us
  blocking collectives  175 us (56%)
  matrix products  66.6 us (21%)
  local copies, waits for them, and re-layouts  24.2 us (8%)
  loops' own time  13.7 us (4%)
  between operations  13.7 us (4%)
  starting transfers between devices  13.2 us (4%)
  other arithmetic  4.5 us (1%)
    psum x3, blocking collectives, operate(): subtree_total = lax.psum(upward, 'leaf')  79.1 us
    dot_general x18, matrix products, near_slot(): product = jnp.einsum('vlp,lpq->lvq', source_vecs, kernel, precision=highest)  50 us
    psum x1, blocking collectives, on_device(): lax.psum(jnp.sum(term_three * term_three, axis=1), ('grp', 'leaf'))  46.5 us
    all_gather x1, blocking collectives, on_device(): subtree_skel = lax.all_gather(skel_points, 'leaf', axis=0, tiled=True)  21.1 us
    all_gather x1, blocking collectives, on_device(): subtree_lists = lax.all_gather(inter_lists, 'leaf', axis=0, tiled=True)  15.5 us
    another operation x3, loops' own time, operate(): lax.fori_loop(0, live_slots, near_slot, jnp.zeros((per_dev, vec_count, le...  13.7 us
    all_gather x3, blocking collectives, operate(): lax.all_gather(subtree_total[None], 'grp', axis=0, tiled=True)  13.1 us
    dot_general x3, matrix products, operate(): jnp.einsum('jvr,tjrq->tvq', coeffs, push_kernel, precision=highest)  10.4 us
  transfers between devices with their start and end apart: 9, of which 2 were waited for; matrix products, arithmetic and copies ran while one was open for 29% of the time, Pallas kernels for 0%

commit v1 on v0

--- a/solution.py
+++ b/solution.py
@@ -92,7 +92,9 @@
     term_one = (operate(vectors) - centre * vectors) / half_width
     term_two = 2.0 * (operate(term_one) - centre * term_one) / half_width - vectors
     term_three = 2.0 * (operate(term_two) - centre * term_two) / half_width - term_one
-    squares = lax.psum(jnp.sum(term_three * term_three, axis=1), ("grp", "leaf"))
+    squares = jnp.sum(
+        lax.all_gather(jnp.sum(term_three * term_three, axis=1), ("grp", "leaf")), axis=0
+    )
     total_points = vectors.shape[1] * group_count * lax.axis_size("leaf")
     return term_three / jnp.sqrt(squares / total_points + 1e-06)[:, None]
 

time: 313 us -> 315 us (level)
    unnamed x0 -> x1, blocking collectives: none -> 46.9 us
    psum x1 -> x0, blocking collectives: 46.5 us -> none  [on_device(): lax.psum(jnp.sum(term_three * term_three, axis=1), ('grp', 'leaf'))]
  transfers between devices with their start and end apart: 9 -> 9, of which waited for: 2 -> 2; matrix products, arithmetic and copies ran while one was open for 29% -> 28% of each run, Pallas kernels for 0% -> 0%
where the time goes in v1:
time: 315 us; the launch traced here: 314 us
  blocking collectives  176 us (56%)
  matrix products  66.6 us (21%)
  local copies, waits for them, and re-layouts  24.5 us (8%)
  loops' own time  14.7 us (5%)
  between operations  13.7 us (4%)
  starting transfers between devices  13.2 us (4%)
  other arithmetic  4.59 us (1%)
    psum x3, blocking collectives, operate(): subtree_total = lax.psum(upward, 'leaf')  79.4 us
    dot_general x18, matrix products, near_slot(): product = jnp.einsum('vlp,lpq->lvq', source_vecs, kernel, precision=highest)  50 us
    unnamed x1, blocking collectives  46.9 us
    all_gather x1, blocking collectives, on_device(): subtree_skel = lax.all_gather(skel_points, 'leaf', axis=0, tiled=True)  21.1 us
    all_gather x1, blocking collectives, on_device(): subtree_lists = lax.all_gather(inter_lists, 'leaf', axis=0, tiled=True)  15.5 us
    another operation x3, loops' own time, operate(): lax.fori_loop(0, live_slots, near_slot, jnp.zeros((per_dev, vec_count, le...  14.7 us
    all_gather x3, blocking collectives, operate(): lax.all_gather(subtree_total[None], 'grp', axis=0, tiled=True)  13.1 us
    dot_general x3, matrix products, operate(): jnp.einsum('jvr,tjrq->tvq', coeffs, push_kernel, precision=highest)  10.4 us
  transfers between devices with their start and end apart: 9, of which 2 were waited for; matrix products, arithmetic and copies ran while one was open for 28% of the time, Pallas kernels for 0%

profile of v1, /device:TPU:10, one launch (start us, length us, event | category | flops | bytes accessed | tf_op | source)
XLA Modules:
  0.0 313.9 jit_solution(5129793640773442072)
XLA Ops:
  6.5 0.9 pad_maximum_fusion.3
  7.5 2.1 collective-permute-start.1
  9.5 2.4 collective-permute-start
  11.9 0.9 copy.61
  13.0 1.2 gather_fusion.6
  14.4 15.5 %all-gather.1 = s32[16,2,16]{2,1,0:T(2,128)S(1)} all-gather(s32[1,2,16]{2,1,0:T(2,128)S(1)} %bitcast.260), channel_id=1, replica_groups=mesh['grp'=2,'leaf'=16] {'leaf'}, dimensions={0}, use_global_device_ids=true | all-gather | bytes 2176 | tf_op jit(solution)/shard_map/all_gather | solution.py:49
  30.1 21.1 %all_gather.21 = f32[32,3,64]{2,1,0:T(4,128)S(1)} all-gather(f32[2,3,64]{2,1,0:T(4,128)S(1)} %bitcast_select_fusion.1), channel_id=1, replica_groups=mesh['grp'=2,'leaf'=16] {'leaf'}, dimensions={0}, use_global_device_ids=true | all-gather | bytes 26112 | tf_op jit(solution)/shard_map/all_gather | solution.py:43
  51.6 3.5 %convolution_bitcast_fusion.2 = f32[32,16,64]{2,1,0:T(8,128)} fusion(f32[32,2]{1,0:T(8,128)S(1)} %copy.67, f32[32,64]{1,0:T(8,128)S(1)} %bitcast.254, f32[2,64]{1,0:T(2,128)S(1)} %bitcast.264, f32[32,64]{1,0:T(8,128)S(1)} %bitcast.257, f32[2,64]{1,0:T(2,128)S(1)} %bitcast.267, f32[32,64]{1,0:T(8,128)S(1)} %bitcast.251, f32[2,64]{1,0:T(2,128)S(1)} %bitcast.261, ...), kind=kOutput, calls=%fused_computation.145 | convolution fusion | flops 53739520 | bytes 165632 | tf_op jit(solution)/shard_map/jvr,tjrq->tvq/dot_general | solution.py:78
  56.1 24.3 %psum.21 = f32[1,16,128]{2,1,0:T(8,128)S(1)} all-reduce(f32[1,16,128]{2,1,0:T(8,128)S(1)} %convolution_bitcast_fusion.8), channel_id=1, replica_groups=mesh['grp'=2,'leaf'=16] {'leaf'}, use_global_device_ids=true, to_apply=%region_6.9 | all-reduce | flops 2048 | bytes 16384 | tf_op jit(solution)/shard_map/psum | solution.py:84
  80.4 4.4 %all_gather.23 = f32[2,16,128]{2,1,0:T(8,128)S(1)} all-gather(f32[1,16,128]{2,1,0:T(8,128)S(1)} %psum.21), channel_id=1, replica_groups=mesh['grp'=2,'leaf'=16] {'grp'}, dimensions={0}, use_global_device_ids=true | all-gather | bytes 24576 | tf_op jit(solution)/shard_map/all_gather | solution.py:85
  85.3 0.7 reduce_max.9
  86.1 29.0 %while.30 = (s32[]{:T(128)}, f32[2,16,512]{2,1,0:T(8,128)S(1)}, s32[]{:T(128)}, s32[2,6]{0,1:T(8,128)S(1)}, f32[16,6,512]{2,0,1:T(8,128)S(1)}, /*index=5*/f32[3,...) while((s32[]{:T(128)}, f32[2,16,512]{2,1,0:T(8,128)S(1)}, s32[]{:T(128)}, ...), condition=%wide.region_3.0_spmd, body=%wide.region_2.0_spmd.sunk | while | flops 107008024 | bytes 479441 | solution.py:72
  88.0 2.8 fusion.199
  92.8 2.8 fusion.199
  97.5 2.8 fusion.199
  102.2 2.8 fusion.199
  107.0 2.8 fusion.199
  110.4 0.6 gather_fusion
  111.7 2.8 fusion.199
  115.1 0.9 fusion.116
  116.4 1.9 collective-permute-start.3
  118.4 2.4 collective-permute-start.2
  121.1 3.5 %convolution_bitcast_fusion.1 = f32[32,16,64]{2,1,0:T(8,128)} fusion(f32[32,2]{1,0:T(8,128)S(1)} %copy.67, f32[32,64]{1,0:T(8,128)S(1)} %bitcast.255, f32[2,64]{1,0:T(2,128)S(1)} %bitcast.265, f32[32,64]{1,0:T(8,128)S(1)} %bitcast.258, f32[2,64]{1,0:T(2,128)S(1)} %bitcast.268, f32[32,64]{1,0:T(8,128)S(1)} %bitcast.252, f32[2,64]{1,0:T(2,128)S(1)} %bitcast.262, ...), kind=kOutput, calls=%fused_computation.144 | convolution fusion | flops 53739520 | bytes 165632 | tf_op jit(solution)/shard_map/jvr,tjrq->tvq/dot_general | solution.py:78
  124.9 26.7 %psum.22 = f32[1,16,128]{2,1,0:T(8,128)S(1)} all-reduce(f32[1,16,128]{2,1,0:T(8,128)S(1)} %convolution_bitcast_fusion.7), channel_id=1, replica_groups=mesh['grp'=2,'leaf'=16] {'leaf'}, use_global_device_ids=true, to_apply=%region_10.13 | all-reduce | flops 2048 | bytes 16384 | tf_op jit(solution)/shard_map/psum | solution.py:84
  151.6 4.4 %all_gather.24 = f32[2,16,128]{2,1,0:T(8,128)S(1)} all-gather(f32[1,16,128]{2,1,0:T(8,128)S(1)} %psum.22), channel_id=1, replica_groups=mesh['grp'=2,'leaf'=16] {'grp'}, dimensions={0}, use_global_device_ids=true | all-gather | bytes 24576 | tf_op jit(solution)/shard_map/all_gather | solution.py:85
  156.4 29.2 %while.31 = (s32[]{:T(128)}, f32[2,16,512]{2,1,0:T(8,128)S(1)}, s32[]{:T(128)}, s32[2,6]{0,1:T(8,128)S(1)}, f32[16,6,512]{2,0,1:T(8,128)S(1)}, /*index=5*/f32[3,...) while((s32[]{:T(128)}, f32[2,16,512]{2,1,0:T(8,128)S(1)}, s32[]{:T(128)}, ...), condition=%wide.region_8.11_spmd, body=%wide.region_7.10_spmd.sunk | while | flops 107008024 | bytes 479441 | solution.py:72
  158.6 2.8 fusion.203
  163.3 2.8 fusion.203
  168.0 2.8 fusion.203
  172.7 2.8 fusion.203
  177.5 2.8 fusion.203
  182.2 2.8 fusion.203
  185.7 0.9 fusion.115
  187.0 1.9 collective-permute-start.5
  189.0 2.4 collective-permute-start.4
  191.7 3.5 %convolution_bitcast_fusion = f32[32,16,64]{2,1,0:T(8,128)} fusion(f32[32,2]{1,0:T(8,128)S(1)} %copy.67, f32[32,64]{1,0:T(8,128)S(1)} %bitcast.256, f32[2,64]{1,0:T(2,128)S(1)} %bitcast.266, f32[32,64]{1,0:T(8,128)S(1)} %bitcast.259, f32[2,64]{1,0:T(2,128)S(1)} %bitcast.269, f32[32,64]{1,0:T(8,128)S(1)} %bitcast.253, f32[2,64]{1,0:T(2,128)S(1)} %bitcast.263, ...), kind=kOutput, calls=%fused_computation.143 | convolution fusion | flops 53739520 | bytes 165632 | tf_op jit(solution)/shard_map/jvr,tjrq->tvq/dot_general | solution.py:78
  195.4 28.5 %psum.23 = f32[1,16,128]{2,1,0:T(8,128)S(1)} all-reduce(f32[1,16,128]{2,1,0:T(8,128)S(1)} %convolution_bitcast_fusion.6), channel_id=1, replica_groups=mesh['grp'=2,'leaf'=16] {'leaf'}, use_global_device_ids=true, to_apply=%region_14.17 | all-reduce | flops 2048 | bytes 16384 | tf_op jit(solution)/shard_map/psum | solution.py:84
  223.9 4.4 %all_gather.25 = f32[2,16,128]{2,1,0:T(8,128)S(1)} all-gather(f32[1,16,128]{2,1,0:T(8,128)S(1)} %psum.23), channel_id=1, replica_groups=mesh['grp'=2,'leaf'=16] {'grp'}, dimensions={0}, use_global_device_ids=true | all-gather | bytes 24576 | tf_op jit(solution)/shard_map/all_gather | solution.py:85
  228.7 29.0 %while.32 = (s32[]{:T(128)}, f32[2,16,512]{2,1,0:T(8,128)S(1)}, s32[]{:T(128)}, s32[2,6]{0,1:T(8,128)S(1)}, f32[16,6,512]{2,0,1:T(8,128)S(1)}, /*index=5*/f32[3,...) while((s32[]{:T(128)}, f32[2,16,512]{2,1,0:T(8,128)S(1)}, s32[]{:T(128)}, ...), condition=%wide.region_12.15_spmd, body=%wide.region_11.14_spmd.sunk | while | flops 107008024 | bytes 479441 | solution.py:72
  230.6 2.8 fusion.207
  235.4 2.8 fusion.207
  240.1 2.8 fusion.207
  244.8 2.8 fusion.207
  249.6 2.8 fusion.207
  254.3 2.8 fusion.207
  258.1 0.9 fusion.114
  259.7 46.9 %all-reduce = f32[512]{0:T(512)S(1)} all-reduce(f32[512]{0:T(512)S(1)} %dynamic-update-slice), channel_id=2, replica_groups=mesh['grp'=2,'leaf'=16] {'grp','leaf'}, use_global_device_ids=true, to_apply=%add | all-reduce | flops 512 | bytes 4096
  306.7 0.7 broadcast_divide_fusion
  (232 shorter events, 28.1 us)
Async XLA Ops:
  6.5 44.8 %copy-start = (f32[2,64,512]{2,1,0:T(8,128)S(1)}, f32[2,64,512]{2,1,0:T(8,128)}, u32[]{:S(2)}) copy-start(f32[2,64,512]{2,1,0:T(8,128)} %param.23) | copy-start | bytes 786436
  6.5 6.4 %copy-start.7 = (s32[2,64]{1,0:T(2,128)S(1)}, s32[2,64]{1,0:T(2,128)}, u32[]{:S(2)}) copy-start(s32[2,64]{1,0:T(2,128)} %param.22) | copy-start | bytes 1540
  6.5 7.8 %copy-start.5 = (s32[2,16]{1,0:T(2,128)S(1)}, s32[2,16]{1,0:T(2,128)}, u32[]{:S(2)}) copy-start(s32[2,16]{1,0:T(2,128)} %param.21) | copy-start | bytes 388
  6.5 108.6 %reduce-scatter.4.cloned.1.call-start = ((), (), s32[]{:S(2)}) async-start(), calls=%async_computation.3 | async-start | bytes 278528 | tf_op jit(solution)/shard_map/reduce_scatter | solution.py:77
  7.5 43.8 %copy-start.2 = (f32[16,1024]{1,0:T(8,128)S(1)}, f32[16,1024]{1,0:T(8,128)}, u32[]{:S(2)}) copy-start(f32[16,1024]{1,0:T(8,128)} %param.18) | copy-start | bytes 196612
  7.5 78.5 %collective-permute-start.1 = (f32[19,1024]{1,0:T(8,128)S(1)}, f32[19,1024]{1,0:T(8,128)S(1)}, u32[]{:S(2)}, u32[]{:S(2)}) collective-permute-start(f32[19,1024]{1,0:T(8,128)S(1)} %pad_maximum_fusion.3), channel_id=1, source_target_pairs={{1,0},{2,1},{3,2},{4,3},{5,4},{6,5},{7,6},{8,7},{9,8},{10,9},{11,1... | collective-permute-start | bytes 233480 | tf_op jit(solution)/shard_map/ppermute | solution.py:20
  9.5 76.5 %collective-permute-start = (f32[19,1024]{1,0:T(8,128)S(1)}, f32[19,1024]{1,0:T(8,128)S(1)}, u32[]{:S(2)}, u32[]{:S(2)}) collective-permute-start(f32[19,1024]{1,0:T(8,128)S(1)} %pad_maximum_fusion.3), channel_id=1, source_target_pairs={{0,1},{1,2},{2,3},{3,4},{4,5},{5,6},{6,7},{7,8},{8,9},{9,10},{10,1... | collective-permute-start | bytes 233480 | tf_op jit(solution)/shard_map/ppermute | solution.py:19
  55.1 0.7 copy-start.6
  55.1 0.9 copy-start.1
  55.1 29.7 %copy-start.4 = (f32[2,3,128]{2,0,1:T(2,128)S(1)}, f32[2,3,128]{2,0,1:T(2,128)}, u32[]{:S(2)}) copy-start(f32[2,3,128]{2,0,1:T(2,128)} %param.25) | copy-start | bytes 9220
  55.1 30.9 %copy-start.3 = (f32[3,1024]{1,0:T(4,128)S(1)}, f32[3,1024]{1,0:T(4,128)}, u32[]{:S(2)}) copy-start(f32[3,1024]{1,0:T(4,128)} %param.19) | copy-start | bytes 36868
  55.1 130.6 %reduce-scatter.6.cloned.1.call-start = ((), (), s32[]{:S(2)}) async-start(), calls=%async_computation.4 | async-start | bytes 278528 | tf_op jit(solution)/shard_map/reduce_scatter | solution.py:77
  116.4 39.9 %collective-permute-start.3 = (f32[19,1024]{1,0:T(8,128)S(1)}, f32[19,1024]{1,0:T(8,128)S(1)}, u32[]{:S(2)}, u32[]{:S(2)}) collective-permute-start(f32[19,1024]{1,0:T(8,128)S(1)} %pad_maximum_fusion.4), channel_id=1, source_target_pairs={{1,0},{2,1},{3,2},{4,3},{5,4},{6,5},{7,6},{8,7},{9,8},{10,9},{11,1... | collective-permute-start | bytes 233480 | tf_op jit(solution)/shard_map/ppermute | solution.py:20
  118.4 38.0 %collective-permute-start.2 = (f32[19,1024]{1,0:T(8,128)S(1)}, f32[19,1024]{1,0:T(8,128)S(1)}, u32[]{:S(2)}, u32[]{:S(2)}) collective-permute-start(f32[19,1024]{1,0:T(8,128)S(1)} %pad_maximum_fusion.4), channel_id=1, source_target_pairs={{0,1},{1,2},{2,3},{3,4},{4,5},{5,6},{6,7},{7,8},{8,9},{9,10},{10,1... | collective-permute-start | bytes 233480 | tf_op jit(solution)/shard_map/ppermute | solution.py:19
  124.8 133.3 %reduce-scatter.8.cloned.1.call-start = ((), (), s32[]{:S(2)}) async-start(), calls=%async_computation.5 | async-start | bytes 278528 | tf_op jit(solution)/shard_map/reduce_scatter | solution.py:77
  187.0 41.6 %collective-permute-start.5 = (f32[19,1024]{1,0:T(8,128)S(1)}, f32[19,1024]{1,0:T(8,128)S(1)}, u32[]{:S(2)}, u32[]{:S(2)}) collective-permute-start(f32[19,1024]{1,0:T(8,128)S(1)} %pad_maximum_fusion.5), channel_id=1, source_target_pairs={{1,0},{2,1},{3,2},{4,3},{5,4},{6,5},{7,6},{8,7},{9,8},{10,9},{11,1... | collective-permute-start | bytes 233480 | tf_op jit(solution)/shard_map/ppermute | solution.py:20
  189.0 39.6 %collective-permute-start.4 = (f32[19,1024]{1,0:T(8,128)S(1)}, f32[19,1024]{1,0:T(8,128)S(1)}, u32[]{:S(2)}, u32[]{:S(2)}) collective-permute-start(f32[19,1024]{1,0:T(8,128)S(1)} %pad_maximum_fusion.5), channel_id=1, source_target_pairs={{0,1},{1,2},{2,3},{3,4},{4,5},{5,6},{6,7},{7,8},{8,9},{9,10},{10,1... | collective-permute-start | bytes 233480 | tf_op jit(solution)/shard_map/ppermute | solution.py:19
Sparse Core Ops, SparseCore 0:
  55.2 56.6 reduce-scatter.3
  124.9 60.7 reduce-scatter.5
  195.5 62.5 reduce-scatter.7
